TPU v7x, 256 devices: a whole 4x4x8 slice. The times are simulated.
256 devices in a mesh: row: 8 (over x, core), col: 32 (over y, z).
Axes of the slice: x: 4, y: 4, z: 8, core: 2. Of those that a mesh axis runs over, the one named last changes fastest.
Arguments:
- upper_panel: float32 [2048, 8192], P('row', 'col')
- lower_panel: float32 [2048, 8192], P('row', 'col')
- pole_values: float32 [2, 8192], P(None, 'col'), may hold values from 0 to 4, as said below
- coupling: float32 [2, 8192], P(None, 'col'), may hold values from -6 to 6
- kept_mask: int32 [2, 8192], P(None, 'col'), may hold values from 0 to 1, as said below
- shifts: float32 [16384], P('col'), may hold values from 0 to 4
- source: int32 [16384], P('col'), may hold values from 0 to 16384, as said below
Outputs:
- vectors: float32 [2, 2048, 16384], P(None, 'row', 'col')
- slab_weight: float32 [16384], P('col')
Inputs may be any that keep to these rules, and one draw needn't show every extreme that they name: source[j] = 16384 marks an undeflated merged column; any other value is the pole whose child column the merged column copies, and no pole is named twice. Each device's 512 merged columns hold from 64 to 384 undeflated columns, and some device holds exactly 384. kept_mask is 0 exactly at the poles named in source. Some device of col holds no deflated pole: every pole of both children that it holds is kept. `pole_values`: every pole lies at least 0.4 / 16384 away from every entry of shifts.
All inputs are finite; a program needn't handle non-finite values.
Results may differ from a plain program's by a relative error of at most 0.0003.
Values sent between devices are 32-bit elements; how exact they have to be, the bound alone decides.
A program may use at most 64 MiB of HBM per device.

v0:
```python
import math
import jax
import jax.numpy as jnp
from jax import lax
from jax.sharding import PartitionSpec as P

N1 = 8192
exact_mode = lax.Precision.HIGHEST


def cauchy_block(pole_vals, weights, shift_vals):
    return weights[:, :, None] / (pole_vals[:, :, None] - shift_vals[None, None, :])


def local(upper_panel, lower_panel, pole_values, coupling, kept_mask, shifts, source):
    rows_here = upper_panel.shape[0]
    own_cols = shifts.shape[0]
    weighted = coupling * kept_mask.astype(jnp.float32)
    undeflated = source == 2 * N1
    child_base = jnp.array([0, N1], jnp.int32)
    zeros_acc = jnp.zeros((rows_here, own_cols), jnp.float32)
    pieces = (
        lax.all_gather(upper_panel, "col", axis=1, tiled=True),
        lax.all_gather(lower_panel, "col", axis=1, tiled=True),
        lax.all_gather(pole_values, "col", axis=1, tiled=True),
        lax.all_gather(weighted, "col", axis=1, tiled=True),
    )
    span_cols = math.gcd(pieces[0].shape[1], 1024)

    def advance(number, running):
        window = [
            lax.dynamic_slice_in_dim(member, number * span_cols, span_cols, 1) for member in pieces
        ]
        first_pole = number * span_cols
        cauchy = cauchy_block(window[2], window[3], shifts)
        indices = first_pole + lax.iota(jnp.int32, span_cols)
        one_hot = indices[None, :, None] + child_base[:, None, None] == source[None, None, :]
        basis_tile = jnp.where(undeflated[None, None, :], cauchy, one_hot.astype(jnp.float32))
        upper_acc = running[0] + jnp.dot(
            window[0], basis_tile[0], precision=exact_mode, preferred_element_type=jnp.float32
        )
        lower_acc = running[1] + jnp.dot(
            window[1], basis_tile[1], precision=exact_mode, preferred_element_type=jnp.float32
        )
        return (upper_acc, lower_acc, running[2] + jnp.sum(cauchy * cauchy, axis=(0, 1)))

    upper_acc, lower_acc, norm_sums = lax.fori_loop(
        0,
        pieces[0].shape[1] // span_cols,
        advance,
        (zeros_acc, zeros_acc, jnp.zeros((own_cols,), jnp.float32)),
    )
    scaling = jnp.where(undeflated, lax.rsqrt(norm_sums), 1.0)
    vectors = jnp.stack([upper_acc * scaling[None, :], lower_acc * scaling[None, :]])
    partial_weight = jnp.sum(vectors * vectors, axis=(0, 1))
    slab_weight = lax.psum(partial_weight, "row") / (2 * rows_here * lax.axis_size("row"))
    return (vectors, slab_weight)


def solution(mesh):
    in_specs = (
        P("row", "col"),
        P("row", "col"),
        P(None, "col"),
        P(None, "col"),
        P(None, "col"),
        P("col"),
        P("col"),
    )
    out_specs = (P(None, "row", "col"), P("col"))
    return jax.shard_map(local, mesh=mesh, in_specs=in_specs, out_specs=out_specs, check_vma=False)
```

profile of v0, /device:TPU:1, one launch (start us, length us, event | category | flops | bytes accessed | tf_op | source)
XLA Modules:
  0.0 310.2 jit_solution(16482954497444541827)
XLA Ops:
  7.2 0.0 all-gather.3.cloned.1.call-start
  7.2 0.7 all-gather.3.cloned.1.call-update
  7.9 0.0 all-gather.5.cloned.1.call-start
  7.9 0.7 all-gather.5.cloned.1.call-update
  8.7 0.7 convert_multiply_fusion
  9.4 41.5 %all_gather.13 = f32[2,8192]{1,0:T(2,128)S(1)} all-gather(f32[2,256]{1,0:T(2,128)S(1)} %convert_multiply_fusion), channel_id=1, replica_groups=mesh['row'=8,'col'=32] {'col'}, dimensions={1}, use_global_device_ids=true | all-gather | bytes 67584 | tf_op jit(solution)/shard_map/all_gather | solution.py:26
  50.9 39.2 %all_gather.14 = f32[2,8192]{1,0:T(2,128)S(1)} all-gather(f32[2,256]{1,0:T(2,128)} %param.12), channel_id=1, replica_groups=mesh['row'=8,'col'=32] {'col'}, dimensions={1}, use_global_device_ids=true | all-gather | bytes 67584 | tf_op jit(solution)/shard_map/all_gather | solution.py:25
  90.1 0.7 broadcast_compare_fusion
  90.8 23.1 %all-gather.3.cloned.1.call-done = f32[256,8192]{1,0:T(8,128)} async-done(((f32[256,256]{1,0:T(8,128)}), f32[256,8192]{1,0:T(8,128)}) %all-gather.3.cloned.1.call-update) | async-done | bytes 8388624 | tf_op jit(solution)/shard_map/all_gather | solution.py:23
  113.9 102.9 %all-gather.5.cloned.1.call-done = f32[256,8192]{1,0:T(8,128)} async-done(((f32[256,256]{1,0:T(8,128)}), f32[256,8192]{1,0:T(8,128)}) %all-gather.5.cloned.1.call-update) | async-done | bytes 8388624 | tf_op jit(solution)/shard_map/all_gather | solution.py:24
  216.8 68.3 %while.18 = (s32[]{:T(128)}, f32[256,512]{1,0:T(8,128)S(1)}, f32[256,512]{1,0:T(8,128)S(1)}, f32[512]{0:T(512)S(1)}, f32[256,8192]{1,0:T(8,128)}, /*index=5*/pre...) while((s32[]{:T(128)}, f32[256,512]{1,0:T(8,128)S(1)}, ...), condition=%wide.region_2.3_spmd.clone, body=%wide.region_0.2_spmd.clone.sunk | while | flops 3229093376 | bytes 12669679 | solution.py:47
  216.9 0.1 broadcast_add_fusion.2
  216.9 1.9 multiply_reduce_fusion.3
  218.8 3.3 %fusion.17 = f32[256,512]{1,0:T(8,128)S(1)} fusion(f32[2,1024,512]{2,1,0:T(8,128)S(1)} %get-tuple-element.347, f32[256,8192]{1,0:T(8,128)} %get-tuple-element.389, s32[]{:T(128)S(6)} %select_n.28, f32[256,512]{1,0:T(8,128)S(1)} %get-tuple-element.366, pred[]{:T(512)S(6)} %compare.3), kind=kOutput, calls=%fused_computation.9.clone.1 | convolution fusion | flops 1610874880 | bytes 4194309 | tf_op jit(solution)/shard_map/while/body/eval_jaxpr/dot_general | solution.py:42
  222.1 3.3 %fusion.16 = f32[256,512]{1,0:T(8,128)S(1)} fusion(f32[2,1024,512]{2,1,0:T(8,128)S(1)} %get-tuple-element.347, f32[256,8192]{1,0:T(8,128)} %get-tuple-element.383, s32[]{:T(128)S(6)} %select_n.28, f32[256,512]{1,0:T(8,128)S(1)} %get-tuple-element.365, pred[]{:T(512)S(6)} %compare.3), kind=kOutput, calls=%fused_computation.8.clone.1 | convolution fusion | flops 1610874880 | bytes 4194309 | tf_op jit(solution)/shard_map/while/body/eval_jaxpr/dot_general | solution.py:39
  225.4 0.1 broadcast_add_fusion.2
  225.5 1.9 multiply_reduce_fusion.3
  227.4 3.3 %fusion.17 = f32[256,512]{1,0:T(8,128)S(1)} fusion(f32[2,1024,512]{2,1,0:T(8,128)S(1)} %get-tuple-element.347, f32[256,8192]{1,0:T(8,128)} %get-tuple-element.389, s32[]{:T(128)S(6)} %select_n.28, f32[256,512]{1,0:T(8,128)S(1)} %get-tuple-element.366, pred[]{:T(512)S(6)} %compare.3), kind=kOutput, calls=%fused_computation.9.clone.1 | convolution fusion | flops 1610874880 | bytes 4194309 | tf_op jit(solution)/shard_map/while/body/eval_jaxpr/dot_general | solution.py:42
  230.6 3.3 %fusion.16 = f32[256,512]{1,0:T(8,128)S(1)} fusion(f32[2,1024,512]{2,1,0:T(8,128)S(1)} %get-tuple-element.347, f32[256,8192]{1,0:T(8,128)} %get-tuple-element.383, s32[]{:T(128)S(6)} %select_n.28, f32[256,512]{1,0:T(8,128)S(1)} %get-tuple-element.365, pred[]{:T(512)S(6)} %compare.3), kind=kOutput, calls=%fused_computation.8.clone.1 | convolution fusion | flops 1610874880 | bytes 4194309 | tf_op jit(solution)/shard_map/while/body/eval_jaxpr/dot_general | solution.py:39
  233.9 0.1 broadcast_add_fusion.2
  234.0 1.9 multiply_reduce_fusion.3
  235.9 3.3 %fusion.17 = f32[256,512]{1,0:T(8,128)S(1)} fusion(f32[2,1024,512]{2,1,0:T(8,128)S(1)} %get-tuple-element.347, f32[256,8192]{1,0:T(8,128)} %get-tuple-element.389, s32[]{:T(128)S(6)} %select_n.28, f32[256,512]{1,0:T(8,128)S(1)} %get-tuple-element.366, pred[]{:T(512)S(6)} %compare.3), kind=kOutput, calls=%fused_computation.9.clone.1 | convolution fusion | flops 1610874880 | bytes 4194309 | tf_op jit(solution)/shard_map/while/body/eval_jaxpr/dot_general | solution.py:42
  239.2 3.3 %fusion.16 = f32[256,512]{1,0:T(8,128)S(1)} fusion(f32[2,1024,512]{2,1,0:T(8,128)S(1)} %get-tuple-element.347, f32[256,8192]{1,0:T(8,128)} %get-tuple-element.383, s32[]{:T(128)S(6)} %select_n.28, f32[256,512]{1,0:T(8,128)S(1)} %get-tuple-element.365, pred[]{:T(512)S(6)} %compare.3), kind=kOutput, calls=%fused_computation.8.clone.1 | convolution fusion | flops 1610874880 | bytes 4194309 | tf_op jit(solution)/shard_map/while/body/eval_jaxpr/dot_general | solution.py:39
  242.5 0.1 broadcast_add_fusion.2
  242.6 1.9 multiply_reduce_fusion.3
  244.5 3.3 %fusion.17 = f32[256,512]{1,0:T(8,128)S(1)} fusion(f32[2,1024,512]{2,1,0:T(8,128)S(1)} %get-tuple-element.347, f32[256,8192]{1,0:T(8,128)} %get-tuple-element.389, s32[]{:T(128)S(6)} %select_n.28, f32[256,512]{1,0:T(8,128)S(1)} %get-tuple-element.366, pred[]{:T(512)S(6)} %compare.3), kind=kOutput, calls=%fused_computation.9.clone.1 | convolution fusion | flops 1610874880 | bytes 4194309 | tf_op jit(solution)/shard_map/while/body/eval_jaxpr/dot_general | solution.py:42
  247.7 3.3 %fusion.16 = f32[256,512]{1,0:T(8,128)S(1)} fusion(f32[2,1024,512]{2,1,0:T(8,128)S(1)} %get-tuple-element.347, f32[256,8192]{1,0:T(8,128)} %get-tuple-element.383, s32[]{:T(128)S(6)} %select_n.28, f32[256,512]{1,0:T(8,128)S(1)} %get-tuple-element.365, pred[]{:T(512)S(6)} %compare.3), kind=kOutput, calls=%fused_computation.8.clone.1 | convolution fusion | flops 1610874880 | bytes 4194309 | tf_op jit(solution)/shard_map/while/body/eval_jaxpr/dot_general | solution.py:39
  251.0 0.1 broadcast_add_fusion.2
  251.1 1.9 multiply_reduce_fusion.3
  253.0 3.3 %fusion.17 = f32[256,512]{1,0:T(8,128)S(1)} fusion(f32[2,1024,512]{2,1,0:T(8,128)S(1)} %get-tuple-element.347, f32[256,8192]{1,0:T(8,128)} %get-tuple-element.389, s32[]{:T(128)S(6)} %select_n.28, f32[256,512]{1,0:T(8,128)S(1)} %get-tuple-element.366, pred[]{:T(512)S(6)} %compare.3), kind=kOutput, calls=%fused_computation.9.clone.1 | convolution fusion | flops 1610874880 | bytes 4194309 | tf_op jit(solution)/shard_map/while/body/eval_jaxpr/dot_general | solution.py:42
  256.3 3.3 %fusion.16 = f32[256,512]{1,0:T(8,128)S(1)} fusion(f32[2,1024,512]{2,1,0:T(8,128)S(1)} %get-tuple-element.347, f32[256,8192]{1,0:T(8,128)} %get-tuple-element.383, s32[]{:T(128)S(6)} %select_n.28, f32[256,512]{1,0:T(8,128)S(1)} %get-tuple-element.365, pred[]{:T(512)S(6)} %compare.3), kind=kOutput, calls=%fused_computation.8.clone.1 | convolution fusion | flops 1610874880 | bytes 4194309 | tf_op jit(solution)/shard_map/while/body/eval_jaxpr/dot_general | solution.py:39
  259.6 0.1 broadcast_add_fusion.2
  259.6 1.9 multiply_reduce_fusion.3
  261.5 3.3 %fusion.17 = f32[256,512]{1,0:T(8,128)S(1)} fusion(f32[2,1024,512]{2,1,0:T(8,128)S(1)} %get-tuple-element.347, f32[256,8192]{1,0:T(8,128)} %get-tuple-element.389, s32[]{:T(128)S(6)} %select_n.28, f32[256,512]{1,0:T(8,128)S(1)} %get-tuple-element.366, pred[]{:T(512)S(6)} %compare.3), kind=kOutput, calls=%fused_computation.9.clone.1 | convolution fusion | flops 1610874880 | bytes 4194309 | tf_op jit(solution)/shard_map/while/body/eval_jaxpr/dot_general | solution.py:42
  264.8 3.3 %fusion.16 = f32[256,512]{1,0:T(8,128)S(1)} fusion(f32[2,1024,512]{2,1,0:T(8,128)S(1)} %get-tuple-element.347, f32[256,8192]{1,0:T(8,128)} %get-tuple-element.383, s32[]{:T(128)S(6)} %select_n.28, f32[256,512]{1,0:T(8,128)S(1)} %get-tuple-element.365, pred[]{:T(512)S(6)} %compare.3), kind=kOutput, calls=%fused_computation.8.clone.1 | convolution fusion | flops 1610874880 | bytes 4194309 | tf_op jit(solution)/shard_map/while/body/eval_jaxpr/dot_general | solution.py:39
  268.1 0.1 broadcast_add_fusion.2
  268.2 1.9 multiply_reduce_fusion.3
  270.1 3.3 %fusion.17 = f32[256,512]{1,0:T(8,128)S(1)} fusion(f32[2,1024,512]{2,1,0:T(8,128)S(1)} %get-tuple-element.347, f32[256,8192]{1,0:T(8,128)} %get-tuple-element.389, s32[]{:T(128)S(6)} %select_n.28, f32[256,512]{1,0:T(8,128)S(1)} %get-tuple-element.366, pred[]{:T(512)S(6)} %compare.3), kind=kOutput, calls=%fused_computation.9.clone.1 | convolution fusion | flops 1610874880 | bytes 4194309 | tf_op jit(solution)/shard_map/while/body/eval_jaxpr/dot_general | solution.py:42
  273.3 3.3 %fusion.16 = f32[256,512]{1,0:T(8,128)S(1)} fusion(f32[2,1024,512]{2,1,0:T(8,128)S(1)} %get-tuple-element.347, f32[256,8192]{1,0:T(8,128)} %get-tuple-element.383, s32[]{:T(128)S(6)} %select_n.28, f32[256,512]{1,0:T(8,128)S(1)} %get-tuple-element.365, pred[]{:T(512)S(6)} %compare.3), kind=kOutput, calls=%fused_computation.8.clone.1 | convolution fusion | flops 1610874880 | bytes 4194309 | tf_op jit(solution)/shard_map/while/body/eval_jaxpr/dot_general | solution.py:39
  276.6 0.1 broadcast_add_fusion.2
  276.7 1.9 multiply_reduce_fusion.3
  278.6 3.3 %fusion.17 = f32[256,512]{1,0:T(8,128)S(1)} fusion(f32[2,1024,512]{2,1,0:T(8,128)S(1)} %get-tuple-element.347, f32[256,8192]{1,0:T(8,128)} %get-tuple-element.389, s32[]{:T(128)S(6)} %select_n.28, f32[256,512]{1,0:T(8,128)S(1)} %get-tuple-element.366, pred[]{:T(512)S(6)} %compare.3), kind=kOutput, calls=%fused_computation.9.clone.1 | convolution fusion | flops 1610874880 | bytes 4194309 | tf_op jit(solution)/shard_map/while/body/eval_jaxpr/dot_general | solution.py:42
  281.9 3.3 %fusion.16 = f32[256,512]{1,0:T(8,128)S(1)} fusion(f32[2,1024,512]{2,1,0:T(8,128)S(1)} %get-tuple-element.347, f32[256,8192]{1,0:T(8,128)} %get-tuple-element.383, s32[]{:T(128)S(6)} %select_n.28, f32[256,512]{1,0:T(8,128)S(1)} %get-tuple-element.365, pred[]{:T(512)S(6)} %compare.3), kind=kOutput, calls=%fused_computation.8.clone.1 | convolution fusion | flops 1610874880 | bytes 4194309 | tf_op jit(solution)/shard_map/while/body/eval_jaxpr/dot_general | solution.py:39
  285.2 0.7 rsqrt_select_fusion
  285.8 0.1 multiply_bitcast_fusion.1
  286.0 1.1 multiply_reduce_fusion.1
  287.1 15.6 %psum.7 = f32[512]{0:T(512)S(1)} all-reduce(f32[512]{0:T(512)S(1)} %get-tuple-element.266), channel_id=1, replica_groups=mesh['row'=8,'col'=32] {'row'}, use_global_device_ids=true, to_apply=%region_4.5 | all-reduce | flops 512 | bytes 4096 | tf_op jit(solution)/shard_map/psum | solution.py:56
  302.7 0.6 broadcast_multiply_fusion
  (35 shorter events, 0.2 us)
Async XLA Ops:
  7.2 106.8 %all-gather.3.cloned.1.call-start = ((), (), s32[]{:S(2)}) async-start(), calls=%async_computation | async-start | bytes 8650752 | tf_op jit(solution)/shard_map/all_gather | solution.py:23
  7.9 209.0 %all-gather.5.cloned.1.call-start = ((), (), s32[]{:S(2)}) async-start(), calls=%async_computation.1 | async-start | bytes 8650752 | tf_op jit(solution)/shard_map/all_gather | solution.py:24
Sparse Core Ops, SparseCore 0:
  10.4 103.4 all-gather.2
  116.4 100.4 all-gather.4
where the time goes:
time: 311 us; the launch traced here: 310 us
  waiting for transfers between devices  127 us (41%)
  blocking collectives  96.3 us (31%)
  matrix products  52.1 us (17%)
  other arithmetic  19.7 us (6%)
  between operations  14.1 us (5%)
    all_gather x1, waiting for transfers between devices, local(): lax.all_gather(lower_panel, 'col', axis=1, tiled=True)  103 us
    all_gather x1, blocking collectives, local(): lax.all_gather(weighted, 'col', axis=1, tiled=True)  41.5 us
    all_gather x1, blocking collectives, local(): lax.all_gather(pole_values, 'col', axis=1, tiled=True)  39.2 us
    dot_general x8, matrix products, advance(): jnp.dot(window[0], basis_tile[0], precision=exact_mode, preferred_element...  26 us
    dot_general x8, matrix products, advance(): jnp.dot(window[1], basis_tile[1], precision=exact_mode, preferred_element...  26 us
    all_gather x1, waiting for transfers between devices, local(): lax.all_gather(upper_panel, 'col', axis=1, tiled=True)  23.1 us
    psum x1, blocking collectives, local(): lax.psum(partial_weight, 'row') / (2 * rows_here * lax.axis_size('row'))  15.6 us
    reduce_sum x8, other arithmetic, advance(): jnp.sum(cauchy * cauchy, axis=(0, 1))  15 us
  transfers between devices with their start and end apart: 2, of which 2 were waited for; matrix products, arithmetic and copies ran while one was open for 0% of the time, Pallas kernels for 0%

commit v1 on v0

--- a/solution.py
+++ b/solution.py
@@ -23,7 +23,7 @@
         lax.all_gather(upper_panel, "col", axis=1, tiled=True),
         lax.all_gather(lower_panel, "col", axis=1, tiled=True),
         lax.all_gather(pole_values, "col", axis=1, tiled=True),
-        lax.all_gather(weighted, "col", axis=1, tiled=True),
+        jnp.concatenate(lax.all_gather(weighted, "col"), axis=1),
     )
     span_cols = math.gcd(pieces[0].shape[1], 1024)
 

time: 311 us -> 311 us (level)
  no operation moved by 1% of the time
where the time goes in v1:
time: 311 us; the launch traced here: 310 us
  waiting for transfers between devices  127 us (41%)
  blocking collectives  96.3 us (31%)
  matrix products  52.1 us (17%)
  other arithmetic  19.7 us (6%)
  between operations  14.1 us (5%)
    all_gather x1, waiting for transfers between devices, local(): lax.all_gather(lower_panel, 'col', axis=1, tiled=True)  103 us
    all_gather x1, blocking collectives, local(): lax.all_gather(weighted, 'col')  41.5 us
    all_gather x1, blocking collectives, local(): lax.all_gather(pole_values, 'col', axis=1, tiled=True)  39.2 us
    dot_general x8, matrix products, advance(): jnp.dot(window[0], basis_tile[0], precision=exact_mode, preferred_element...  26 us
    dot_general x8, matrix products, advance(): jnp.dot(window[1], basis_tile[1], precision=exact_mode, preferred_element...  26 us
    all_gather x1, waiting for transfers between devices, local(): lax.all_gather(upper_panel, 'col', axis=1, tiled=True)  23.1 us
    psum x1, blocking collectives, local(): lax.psum(partial_weight, 'row') / (2 * rows_here * lax.axis_size('row'))  15.6 us
    reduce_sum x8, other arithmetic, advance(): jnp.sum(cauchy * cauchy, axis=(0, 1))  15 us
  transfers between devices with their start and end apart: 2, of which 2 were waited for; matrix products, arithmetic and copies ran while one was open for 0% of the time, Pallas kernels for 0%

profile of v1, /device:TPU:1, one launch (start us, length us, event | category | flops | bytes accessed | tf_op | source)
XLA Modules:
  0.0 310.2 jit_solution(17021202918650420559)
XLA Ops:
  7.2 0.0 all-gather.5.cloned.1.call-start
  7.2 0.7 all-gather.5.cloned.1.call-update
  7.9 0.0 all-gather.7.cloned.1.call-start
  7.9 0.7 all-gather.7.cloned.1.call-update
  8.7 0.7 multiply_bitcast_fusion.2
  9.4 41.5 %all-gather.1 = f32[32,2,256]{2,1,0:T(2,128)S(1)} all-gather(f32[1,2,256]{2,1,0:T(2,128)S(1)} %multiply_bitcast_fusion.2), channel_id=2, replica_groups=mesh['row'=8,'col'=32] {'col'}, dimensions={0}, use_global_device_ids=true | all-gather | bytes 67584 | tf_op jit(solution)/shard_map/all_gather | solution.py:26
  50.9 39.2 %all_gather.18 = f32[2,8192]{1,0:T(2,128)S(1)} all-gather(f32[2,256]{1,0:T(2,128)} %param.12), channel_id=1, replica_groups=mesh['row'=8,'col'=32] {'col'}, dimensions={1}, use_global_device_ids=true | all-gather | bytes 67584 | tf_op jit(solution)/shard_map/all_gather | solution.py:25
  90.1 0.7 broadcast_compare_fusion
  90.8 23.1 %all-gather.5.cloned.1.call-done = f32[256,8192]{1,0:T(8,128)} async-done(((f32[256,256]{1,0:T(8,128)}), f32[256,8192]{1,0:T(8,128)}) %all-gather.5.cloned.1.call-update) | async-done | bytes 8388624 | tf_op jit(solution)/shard_map/all_gather | solution.py:23
  113.9 102.9 %all-gather.7.cloned.1.call-done = f32[256,8192]{1,0:T(8,128)} async-done(((f32[256,256]{1,0:T(8,128)}), f32[256,8192]{1,0:T(8,128)}) %all-gather.7.cloned.1.call-update) | async-done | bytes 8388624 | tf_op jit(solution)/shard_map/all_gather | solution.py:24
  216.8 68.3 %while.18 = (s32[]{:T(128)}, f32[256,512]{1,0:T(8,128)S(1)}, f32[256,512]{1,0:T(8,128)S(1)}, f32[512]{0:T(512)S(1)}, f32[256,8192]{1,0:T(8,128)}, /*index=5*/pre...) while((s32[]{:T(128)}, f32[256,512]{1,0:T(8,128)S(1)}, ...), condition=%wide.region_2.3_spmd.clone, body=%wide.region_0.2_spmd.clone.sunk | while | flops 3229093376 | bytes 12669679 | solution.py:47
  216.9 0.1 broadcast_add_fusion.2
  216.9 1.9 multiply_reduce_fusion.3
  218.8 3.3 %fusion.17 = f32[256,512]{1,0:T(8,128)S(1)} fusion(f32[2,1024,512]{2,1,0:T(8,128)S(1)} %get-tuple-element.347, f32[256,8192]{1,0:T(8,128)} %get-tuple-element.389, s32[]{:T(128)S(6)} %select_n.28, f32[256,512]{1,0:T(8,128)S(1)} %get-tuple-element.366, pred[]{:T(512)S(6)} %compare.3), kind=kOutput, calls=%fused_computation.9.clone.1 | convolution fusion | flops 1610874880 | bytes 4194309 | tf_op jit(solution)/shard_map/while/body/eval_jaxpr/dot_general | solution.py:42
  222.1 3.3 %fusion.16 = f32[256,512]{1,0:T(8,128)S(1)} fusion(f32[2,1024,512]{2,1,0:T(8,128)S(1)} %get-tuple-element.347, f32[256,8192]{1,0:T(8,128)} %get-tuple-element.383, s32[]{:T(128)S(6)} %select_n.28, f32[256,512]{1,0:T(8,128)S(1)} %get-tuple-element.365, pred[]{:T(512)S(6)} %compare.3), kind=kOutput, calls=%fused_computation.8.clone.1 | convolution fusion | flops 1610874880 | bytes 4194309 | tf_op jit(solution)/shard_map/while/body/eval_jaxpr/dot_general | solution.py:39
  225.4 0.1 broadcast_add_fusion.2
  225.5 1.9 multiply_reduce_fusion.3
  227.4 3.3 %fusion.17 = f32[256,512]{1,0:T(8,128)S(1)} fusion(f32[2,1024,512]{2,1,0:T(8,128)S(1)} %get-tuple-element.347, f32[256,8192]{1,0:T(8,128)} %get-tuple-element.389, s32[]{:T(128)S(6)} %select_n.28, f32[256,512]{1,0:T(8,128)S(1)} %get-tuple-element.366, pred[]{:T(512)S(6)} %compare.3), kind=kOutput, calls=%fused_computation.9.clone.1 | convolution fusion | flops 1610874880 | bytes 4194309 | tf_op jit(solution)/shard_map/while/body/eval_jaxpr/dot_general | solution.py:42
  230.6 3.3 %fusion.16 = f32[256,512]{1,0:T(8,128)S(1)} fusion(f32[2,1024,512]{2,1,0:T(8,128)S(1)} %get-tuple-element.347, f32[256,8192]{1,0:T(8,128)} %get-tuple-element.383, s32[]{:T(128)S(6)} %select_n.28, f32[256,512]{1,0:T(8,128)S(1)} %get-tuple-element.365, pred[]{:T(512)S(6)} %compare.3), kind=kOutput, calls=%fused_computation.8.clone.1 | convolution fusion | flops 1610874880 | bytes 4194309 | tf_op jit(solution)/shard_map/while/body/eval_jaxpr/dot_general | solution.py:39
  233.9 0.1 broadcast_add_fusion.2
  234.0 1.9 multiply_reduce_fusion.3
  235.9 3.3 %fusion.17 = f32[256,512]{1,0:T(8,128)S(1)} fusion(f32[2,1024,512]{2,1,0:T(8,128)S(1)} %get-tuple-element.347, f32[256,8192]{1,0:T(8,128)} %get-tuple-element.389, s32[]{:T(128)S(6)} %select_n.28, f32[256,512]{1,0:T(8,128)S(1)} %get-tuple-element.366, pred[]{:T(512)S(6)} %compare.3), kind=kOutput, calls=%fused_computation.9.clone.1 | convolution fusion | flops 1610874880 | bytes 4194309 | tf_op jit(solution)/shard_map/while/body/eval_jaxpr/dot_general | solution.py:42
  239.2 3.3 %fusion.16 = f32[256,512]{1,0:T(8,128)S(1)} fusion(f32[2,1024,512]{2,1,0:T(8,128)S(1)} %get-tuple-element.347, f32[256,8192]{1,0:T(8,128)} %get-tuple-element.383, s32[]{:T(128)S(6)} %select_n.28, f32[256,512]{1,0:T(8,128)S(1)} %get-tuple-element.365, pred[]{:T(512)S(6)} %compare.3), kind=kOutput, calls=%fused_computation.8.clone.1 | convolution fusion | flops 1610874880 | bytes 4194309 | tf_op jit(solution)/shard_map/while/body/eval_jaxpr/dot_general | solution.py:39
  242.5 0.1 broadcast_add_fusion.2
  242.6 1.9 multiply_reduce_fusion.3
  244.5 3.3 %fusion.17 = f32[256,512]{1,0:T(8,128)S(1)} fusion(f32[2,1024,512]{2,1,0:T(8,128)S(1)} %get-tuple-element.347, f32[256,8192]{1,0:T(8,128)} %get-tuple-element.389, s32[]{:T(128)S(6)} %select_n.28, f32[256,512]{1,0:T(8,128)S(1)} %get-tuple-element.366, pred[]{:T(512)S(6)} %compare.3), kind=kOutput, calls=%fused_computation.9.clone.1 | convolution fusion | flops 1610874880 | bytes 4194309 | tf_op jit(solution)/shard_map/while/body/eval_jaxpr/dot_general | solution.py:42
  247.7 3.3 %fusion.16 = f32[256,512]{1,0:T(8,128)S(1)} fusion(f32[2,1024,512]{2,1,0:T(8,128)S(1)} %get-tuple-element.347, f32[256,8192]{1,0:T(8,128)} %get-tuple-element.383, s32[]{:T(128)S(6)} %select_n.28, f32[256,512]{1,0:T(8,128)S(1)} %get-tuple-element.365, pred[]{:T(512)S(6)} %compare.3), kind=kOutput, calls=%fused_computation.8.clone.1 | convolution fusion | flops 1610874880 | bytes 4194309 | tf_op jit(solution)/shard_map/while/body/eval_jaxpr/dot_general | solution.py:39
  251.0 0.1 broadcast_add_fusion.2
  251.1 1.9 multiply_reduce_fusion.3
  253.0 3.3 %fusion.17 = f32[256,512]{1,0:T(8,128)S(1)} fusion(f32[2,1024,512]{2,1,0:T(8,128)S(1)} %get-tuple-element.347, f32[256,8192]{1,0:T(8,128)} %get-tuple-element.389, s32[]{:T(128)S(6)} %select_n.28, f32[256,512]{1,0:T(8,128)S(1)} %get-tuple-element.366, pred[]{:T(512)S(6)} %compare.3), kind=kOutput, calls=%fused_computation.9.clone.1 | convolution fusion | flops 1610874880 | bytes 4194309 | tf_op jit(solution)/shard_map/while/body/eval_jaxpr/dot_general | solution.py:42
  256.3 3.3 %fusion.16 = f32[256,512]{1,0:T(8,128)S(1)} fusion(f32[2,1024,512]{2,1,0:T(8,128)S(1)} %get-tuple-element.347, f32[256,8192]{1,0:T(8,128)} %get-tuple-element.383, s32[]{:T(128)S(6)} %select_n.28, f32[256,512]{1,0:T(8,128)S(1)} %get-tuple-element.365, pred[]{:T(512)S(6)} %compare.3), kind=kOutput, calls=%fused_computation.8.clone.1 | convolution fusion | flops 1610874880 | bytes 4194309 | tf_op jit(solution)/shard_map/while/body/eval_jaxpr/dot_general | solution.py:39
  259.6 0.1 broadcast_add_fusion.2
  259.6 1.9 multiply_reduce_fusion.3
  261.5 3.3 %fusion.17 = f32[256,512]{1,0:T(8,128)S(1)} fusion(f32[2,1024,512]{2,1,0:T(8,128)S(1)} %get-tuple-element.347, f32[256,8192]{1,0:T(8,128)} %get-tuple-element.389, s32[]{:T(128)S(6)} %select_n.28, f32[256,512]{1,0:T(8,128)S(1)} %get-tuple-element.366, pred[]{:T(512)S(6)} %compare.3), kind=kOutput, calls=%fused_computation.9.clone.1 | convolution fusion | flops 1610874880 | bytes 4194309 | tf_op jit(solution)/shard_map/while/body/eval_jaxpr/dot_general | solution.py:42
  264.8 3.3 %fusion.16 = f32[256,512]{1,0:T(8,128)S(1)} fusion(f32[2,1024,512]{2,1,0:T(8,128)S(1)} %get-tuple-element.347, f32[256,8192]{1,0:T(8,128)} %get-tuple-element.383, s32[]{:T(128)S(6)} %select_n.28, f32[256,512]{1,0:T(8,128)S(1)} %get-tuple-element.365, pred[]{:T(512)S(6)} %compare.3), kind=kOutput, calls=%fused_computation.8.clone.1 | convolution fusion | flops 1610874880 | bytes 4194309 | tf_op jit(solution)/shard_map/while/body/eval_jaxpr/dot_general | solution.py:39
  268.1 0.1 broadcast_add_fusion.2
  268.2 1.9 multiply_reduce_fusion.3
  270.1 3.3 %fusion.17 = f32[256,512]{1,0:T(8,128)S(1)} fusion(f32[2,1024,512]{2,1,0:T(8,128)S(1)} %get-tuple-element.347, f32[256,8192]{1,0:T(8,128)} %get-tuple-element.389, s32[]{:T(128)S(6)} %select_n.28, f32[256,512]{1,0:T(8,128)S(1)} %get-tuple-element.366, pred[]{:T(512)S(6)} %compare.3), kind=kOutput, calls=%fused_computation.9.clone.1 | convolution fusion | flops 1610874880 | bytes 4194309 | tf_op jit(solution)/shard_map/while/body/eval_jaxpr/dot_general | solution.py:42
  273.3 3.3 %fusion.16 = f32[256,512]{1,0:T(8,128)S(1)} fusion(f32[2,1024,512]{2,1,0:T(8,128)S(1)} %get-tuple-element.347, f32[256,8192]{1,0:T(8,128)} %get-tuple-element.383, s32[]{:T(128)S(6)} %select_n.28, f32[256,512]{1,0:T(8,128)S(1)} %get-tuple-element.365, pred[]{:T(512)S(6)} %compare.3), kind=kOutput, calls=%fused_computation.8.clone.1 | convolution fusion | flops 1610874880 | bytes 4194309 | tf_op jit(solution)/shard_map/while/body/eval_jaxpr/dot_general | solution.py:39
  276.6 0.1 broadcast_add_fusion.2
  276.7 1.9 multiply_reduce_fusion.3
  278.6 3.3 %fusion.17 = f32[256,512]{1,0:T(8,128)S(1)} fusion(f32[2,1024,512]{2,1,0:T(8,128)S(1)} %get-tuple-element.347, f32[256,8192]{1,0:T(8,128)} %get-tuple-element.389, s32[]{:T(128)S(6)} %select_n.28, f32[256,512]{1,0:T(8,128)S(1)} %get-tuple-element.366, pred[]{:T(512)S(6)} %compare.3), kind=kOutput, calls=%fused_computation.9.clone.1 | convolution fusion | flops 1610874880 | bytes 4194309 | tf_op jit(solution)/shard_map/while/body/eval_jaxpr/dot_general | solution.py:42
  281.9 3.3 %fusion.16 = f32[256,512]{1,0:T(8,128)S(1)} fusion(f32[2,1024,512]{2,1,0:T(8,128)S(1)} %get-tuple-element.347, f32[256,8192]{1,0:T(8,128)} %get-tuple-element.383, s32[]{:T(128)S(6)} %select_n.28, f32[256,512]{1,0:T(8,128)S(1)} %get-tuple-element.365, pred[]{:T(512)S(6)} %compare.3), kind=kOutput, calls=%fused_computation.8.clone.1 | convolution fusion | flops 1610874880 | bytes 4194309 | tf_op jit(solution)/shard_map/while/body/eval_jaxpr/dot_general | solution.py:39
  285.2 0.7 rsqrt_select_fusion
  285.8 0.1 multiply_bitcast_fusion.1
  286.0 1.1 multiply_reduce_fusion.1
  287.1 15.6 %psum.7 = f32[512]{0:T(512)S(1)} all-reduce(f32[512]{0:T(512)S(1)} %get-tuple-element.266), channel_id=1, replica_groups=mesh['row'=8,'col'=32] {'row'}, use_global_device_ids=true, to_apply=%region_4.5 | all-reduce | flops 512 | bytes 4096 | tf_op jit(solution)/shard_map/psum | solution.py:56
  302.7 0.6 broadcast_multiply_fusion
  (35 shorter events, 0.2 us)
Async XLA Ops:
  7.2 106.8 %all-gather.5.cloned.1.call-start = ((), (), s32[]{:S(2)}) async-start(), calls=%async_computation | async-start | bytes 8650752 | tf_op jit(solution)/shard_map/all_gather | solution.py:23
  7.9 209.0 %all-gather.7.cloned.1.call-start = ((), (), s32[]{:S(2)}) async-start(), calls=%async_computation.1 | async-start | bytes 8650752 | tf_op jit(solution)/shard_map/all_gather | solution.py:24
Sparse Core Ops, SparseCore 0:
  10.4 103.4 all-gather.4
  116.4 100.4 all-gather.6
